TPU v7x, 32 devices: a whole 2x2x4 slice. The times are simulated.
32 devices in a mesh: fsdp: 8 (over y, x, core), sp: 4 (over z).
Axes of the slice: x: 2, y: 2, z: 4, core: 2. Of those that a mesh axis runs over, the one named last changes fastest.
Arguments:
- tokens_in: bfloat16 [8, 1024, 1536], P('fsdp', 'sp')
- w_qkv: bfloat16 [1536, 3, 16, 128], P('fsdp', None, 'sp')
- grad_attn: bfloat16 [8, 1024, 16, 128], P('fsdp', None, 'sp'), may hold values from -6 to 6
- kv_tiles: int32 [16, 8, 4], P('sp'), may hold values from 0 to 7, as said below
- tile_live: int32 [16, 8, 4], P('sp'), may hold values from 0 to 1, as said below
Outputs:
- attention_out: bfloat16 [8, 1024, 16, 128], P('fsdp', None, 'sp')
- grad_tokens: bfloat16 [8, 1024, 1536], P('fsdp', 'sp')
Inputs may be any that keep to these rules, and one draw needn't show every extreme that they name: `kv_tiles`: in every row the first slot names the query tile itself; the live tiles of one row are distinct. `tile_live`: the first slot of every row is live.
All inputs are finite; a program needn't handle non-finite values.
Results may differ from a plain program's by a relative error of at most 0.014.
The roundings to bfloat16 on the way count: a program that leaves them out, or rounds other values in their place, can miss the bound.
Values may be sent and summed in bfloat16 or wider, within the bound.
No kernel may reach another device: no remote copies, remote signals or barrier semaphores. Data moves between devices by JAX's collectives and lax.ppermute only.
A program may use at most 128 MiB of HBM per device.

v0:
```python
import functools

import jax
import jax.numpy as jnp
from jax import lax
from jax.experimental import pallas as pl
from jax.experimental.pallas import tpu as pltpu
from jax.sharding import PartitionSpec as P


HEAD = 128
TILE = 128
NN = (((1,), (0,)), ((), ()))
NT = (((1,), (1,)), ((), ()))


def dot(a, b, dims):
    return lax.dot_general(a, b, dims, preferred_element_type=jnp.float32)


def project_kernel(owner_ref, *refs, shards, parts):
    shard_refs, part_refs = refs[:shards], refs[shards : shards + parts]
    w_ref, qkv_ref, tokens_ref, sems = refs[shards + parts :]
    rows = shard_refs[0].shape[0]
    copies = []
    for number, shard in enumerate(shard_refs):
        at = pl.ds(pl.multiple_of(owner_ref[number] * rows, rows), rows)
        copies.append(pltpu.make_async_copy(shard, w_ref.at[at], sems.at[number]))
    start = 0
    for number, part in enumerate(part_refs):
        at = pl.ds(start, part.shape[0])
        copies.append(pltpu.make_async_copy(part, tokens_ref.at[at], sems.at[shards + number]))
        start += part.shape[0]
    for copy in copies:
        copy.start()
    for copy in copies:
        copy.wait()

    def step(block, carry):
        at = pl.ds(pl.multiple_of(block * TILE, TILE), TILE)
        qkv_ref[at, :] = dot(tokens_ref[at, :], w_ref[...], NN).astype(jnp.bfloat16)
        return carry

    lax.fori_loop(0, start // TILE, step, 0)


def project(owners, shards, parts):
    _, width = shards[0].shape
    depth = parts[0].shape[1]
    length = sum(part.shape[0] for part in parts)
    anywhere = pl.BlockSpec(memory_space=pl.ANY)
    return pl.pallas_call(
        functools.partial(project_kernel, shards=len(shards), parts=len(parts)),
        out_shape=(
            jax.ShapeDtypeStruct((depth, width), jnp.bfloat16),
            jax.ShapeDtypeStruct((length, width), jnp.bfloat16),
        ),
        in_specs=[pl.BlockSpec(memory_space=pltpu.SMEM)] + [anywhere] * (len(shards) + len(parts)),
        out_specs=(pl.BlockSpec(memory_space=pltpu.VMEM),) * 2,
        scratch_shapes=[
            pltpu.VMEM((length, depth), jnp.bfloat16),
            pltpu.SemaphoreType.DMA((len(shards) + len(parts),)),
        ],
        name="project",
        cost_estimate=pl.CostEstimate(
            flops=2 * length * depth * width,
            bytes_accessed=4 * depth * width + 4 * length * width,
            transcendentals=0,
        ),
        compiler_params=pltpu.CompilerParams(vmem_limit_bytes=16 << 20),
    )(owners, *shards, *parts)


def product_kernel(dqkv_ref, w_ref, *out_refs, start):
    for out_ref in out_refs:
        rows = out_ref.shape[0]
        start = start % dqkv_ref.shape[0]
        out_ref[...] = dot(dqkv_ref[start : start + rows, :], w_ref[...], NT)
        start += rows


def products(dqkv, w, start, sizes):
    depth, width = w.shape
    return pl.pallas_call(
        functools.partial(product_kernel, start=start),
        out_shape=tuple(jax.ShapeDtypeStruct((size, depth), jnp.float32) for size in sizes),
        name="products",
        cost_estimate=pl.CostEstimate(
            flops=2 * sum(sizes) * depth * width,
            bytes_accessed=2 * depth * width + 6 * sum(sizes) * depth,
            transcendentals=0,
        ),
        compiler_params=pltpu.CompilerParams(vmem_limit_bytes=20 << 20),
    )(dqkv, w)


def finish_kernel(own_ref, low_ref, high_ref, out_ref):
    half = low_ref.shape[0]
    out_ref[:half, :] = (own_ref[:half, :] + low_ref[...].astype(jnp.float32)).astype(jnp.bfloat16)
    out_ref[half:, :] = (own_ref[half:, :] + high_ref[...].astype(jnp.float32)).astype(jnp.bfloat16)


def finish(own, low, high):
    return pl.pallas_call(
        finish_kernel,
        out_shape=jax.ShapeDtypeStruct(own.shape, jnp.bfloat16),
        name="finish",
        compiler_params=pltpu.CompilerParams(vmem_limit_bytes=8 << 20),
    )(own, low, high)


def attention_kernel(
    place_ref, tiles_ref, live_ref, early_ref, late_ref, last_ref, w_ref, dout_ref,
    out_ref, dqkv_ref, first_ref, second_ref, qkv_ref, kt_ref, vt_ref, dk_ref, dv_ref, sem,
    *, heads, slots, chunk,
):
    length = qkv_ref.shape[0]
    width = heads * HEAD
    tile_count = length // TILE
    scale = HEAD ** (-0.5)
    early = early_ref.shape[0]
    copy = pltpu.make_async_copy(early_ref, qkv_ref.at[pl.ds(0, early)], sem)
    copy.start()
    middle = early + late_ref.shape[0]
    qkv_ref[early:middle, :] = dot(late_ref[...], w_ref[...], NN).astype(jnp.bfloat16)
    qkv_ref[middle:, :] = dot(last_ref[...], w_ref[...], NN).astype(jnp.bfloat16)
    dk_ref[...] = jnp.zeros_like(dk_ref)
    dv_ref[...] = jnp.zeros_like(dv_ref)
    copy.wait()
    for head in range(heads):
        at = head * HEAD
        kt_ref[head] = qkv_ref[:, width + at : width + at + HEAD].T
        vt_ref[head] = qkv_ref[:, 2 * width + at : 2 * width + at + HEAD].T

    def tile_rows(tile):
        return pl.ds(pl.multiple_of(tile * TILE, TILE), TILE)

    def one(head, tile):
        at = head * HEAD
        rows = tile_rows(tile)
        held = tile_rows(place_ref[tile])
        query = qkv_ref[held, at : at + HEAD]
        dout = dout_ref[rows, at : at + HEAD]
        base = (head * tile_count + tile) * slots
        spots = [tile_rows(place_ref[tiles_ref[base + s]]) for s in range(slots)]
        scores = []
        for s in range(slots):
            key = qkv_ref[spots[s], width + at : width + at + HEAD]
            part = dot(key, query, NT) * scale
            scores.append(jnp.where(live_ref[base + s] > 0, part, -1e30))
        peak = jnp.max(functools.reduce(jnp.maximum, scores), axis=0, keepdims=True)
        grown = [jnp.exp(part - peak) for part in scores]
        total = jnp.sum(functools.reduce(jnp.add, grown), axis=0, keepdims=True)
        inverse = 1.0 / total
        probs = [part * inverse for part in grown]
        probs_bf = jnp.concatenate([part.astype(jnp.bfloat16) for part in probs], axis=0)
        grads = []
        for s in range(slots):
            value = qkv_ref[spots[s], 2 * width + at : 2 * width + at + HEAD]
            grads.append(dot(value, dout, NT))
        delta = functools.reduce(jnp.add, [p * g for p, g in zip(probs, grads)])
        delta = jnp.sum(delta, axis=0, keepdims=True)
        dscores = jnp.concatenate(
            [(p * (g - delta) * scale).astype(jnp.bfloat16) for p, g in zip(probs, grads)], axis=0
        )
        value_t = jnp.concatenate([vt_ref[head, :, spot] for spot in spots], axis=1)
        key_t = jnp.concatenate([kt_ref[head, :, spot] for spot in spots], axis=1)
        out_ref[rows, at : at + HEAD] = dot(value_t, probs_bf, NN).T.astype(jnp.bfloat16)
        dqkv_ref[held, at : at + HEAD] = dot(key_t, dscores, NN).T.astype(jnp.bfloat16)
        dk = dot(dscores, query, NN)
        dv = dot(probs_bf, dout, NN)
        for s in range(slots):
            dk_ref[head, spots[s], :] += dk[s * TILE : (s + 1) * TILE]
            dv_ref[head, spots[s], :] += dv[s * TILE : (s + 1) * TILE]

    def step(tile, carry):
        for head in range(heads):
            one(head, tile)
        return carry

    lax.fori_loop(0, tile_count, step, 0)
    for head in range(heads):
        at = head * HEAD
        dqkv_ref[:, width + at : width + at + HEAD] = dk_ref[head].astype(jnp.bfloat16)
        dqkv_ref[:, 2 * width + at : 2 * width + at + HEAD] = dv_ref[head].astype(jnp.bfloat16)


    half = chunk // 2
    first_ref[...] = dot(dqkv_ref[chunk : chunk + half, :], w_ref[...], NT).astype(jnp.bfloat16)
    second_ref[...] = dot(dqkv_ref[chunk + half : 2 * chunk, :], w_ref[...], NT).astype(jnp.bfloat16)


def attention(early, late, last, w, dout, place, kv_tiles, tile_live, chunk):
    length = dout.shape[0]
    heads, tile_count, slots = kv_tiles.shape
    width = heads * HEAD
    depth = w.shape[0]
    smem = pl.BlockSpec(memory_space=pltpu.SMEM)
    vmem = pl.BlockSpec(memory_space=pltpu.VMEM)
    anywhere = pl.BlockSpec(memory_space=pl.ANY)
    return pl.pallas_call(
        functools.partial(attention_kernel, heads=heads, slots=slots, chunk=chunk),
        out_shape=(
            jax.ShapeDtypeStruct((length, width), jnp.bfloat16),
            jax.ShapeDtypeStruct((length, 3 * width), jnp.bfloat16),
            jax.ShapeDtypeStruct((chunk // 2, depth), jnp.bfloat16),
            jax.ShapeDtypeStruct((chunk // 2, depth), jnp.bfloat16),
        ),
        in_specs=[smem, smem, smem, anywhere, vmem, vmem, vmem, vmem],
        out_specs=(vmem, vmem, vmem, vmem),
        scratch_shapes=[
            pltpu.VMEM((length, 3 * width), jnp.bfloat16),
            pltpu.VMEM((heads, HEAD, length), jnp.bfloat16),
            pltpu.VMEM((heads, HEAD, length), jnp.bfloat16),
            pltpu.VMEM((heads, length, HEAD), jnp.float32),
            pltpu.VMEM((heads, length, HEAD), jnp.float32),
            pltpu.SemaphoreType.DMA,
        ],
        name="attention",
        cost_estimate=pl.CostEstimate(
            flops=12 * heads * tile_count * slots * TILE * TILE * HEAD,
            bytes_accessed=16 * length * width,
            transcendentals=heads * tile_count * slots * TILE * TILE,
        ),
        compiler_params=pltpu.CompilerParams(vmem_limit_bytes=26 << 20),
    )(place, kv_tiles.reshape(-1), tile_live.reshape(-1), early, late, last, w, dout)


def folded(count):
    return list(range(0, count, 2)) + list(range(count - 1 - count % 2, 0, -2))


def weight_bits(count):
    return [1 << b for b in range(1, count.bit_length() - 1)]


def gather_weights(w, axis, count):
    half = w.shape[0] // 2

    def swap(value, bit):
        return lax.ppermute(value, axis, [(i, i ^ bit) for i in range(count)])

    held = {0: w}
    bits = weight_bits(count)
    if len(bits) == 2:
        low, high = bits
        held[low] = swap(w, low)
        held[high] = swap(w, high)
        held[low | high] = jnp.concatenate(
            [swap(held[high][:half], low), swap(held[low][half:], high)],
            axis=0,
        )
    else:
        for bit in bits:
            held.update({k | bit: swap(v, bit) for k, v in list(held.items())})
    keys = list(held)
    for k in keys:
        held[k ^ 1] = swap(held[k], 1)
    return held


def make_shards(fsdp_count, sp_count):
    order = folded(sp_count)
    ring = [(order[i], order[(i + 1) % sp_count]) for i in range(sp_count)]
    spot = [order.index(z) for z in range(sp_count)]
    arrived = [[(spot[z] - spot[c]) % sp_count for c in range(sp_count)] for z in range(sp_count)]

    def layer(tokens_in, w_qkv, grad_attn, kv_tiles, tile_live):
        tokens = tokens_in[0]
        chunk, _ = tokens.shape
        half = chunk // 2
        heads, tile_count, _ = kv_tiles.shape
        length = tile_count * TILE
        width = heads * HEAD
        held = gather_weights(w_qkv.reshape(w_qkv.shape[0], -1), "fsdp", fsdp_count)
        halves = [tokens[:half], tokens[half:]]
        parts = [tokens]
        for _ in range(1, sp_count):
            for side in range(2):
                halves[side] = lax.ppermute(halves[side], "sp", ring)
                parts.append(halves[side])
        owners = lax.axis_index("fsdp") ^ jnp.array(list(held), jnp.int32)
        w, early = project(owners, list(held.values()), parts[:-2])
        per_chunk = chunk // TILE
        steps = jnp.array(arrived, jnp.int32)[lax.axis_index("sp")]
        tiles = jnp.arange(tile_count, dtype=jnp.int32)
        place = jnp.repeat(steps, per_chunk) * per_chunk + tiles % per_chunk
        out, dqkv, low, high = attention(
            early, parts[-2], parts[-1], w, grad_attn[0].reshape(length, width), place, kv_tiles, tile_live, chunk
        )
        sums = products(dqkv, w, 2 * chunk, [half] * (2 * (sp_count - 2)) + [chunk])
        for step in range(1, sp_count):
            if step > 1:
                low = (sums[2 * step - 4] + low.astype(jnp.float32)).astype(jnp.bfloat16)
            low = lax.ppermute(low, "sp", ring)
            if step > 1:
                high = (sums[2 * step - 3] + high.astype(jnp.float32)).astype(jnp.bfloat16)
            high = lax.ppermute(high, "sp", ring)
        grad_tokens = finish(sums[-1], low, high)
        return out.reshape(1, length, heads, HEAD), grad_tokens[None]

    return layer


def solution(mesh):
    in_specs = (
        P("fsdp", "sp", None),
        P("fsdp", None, "sp", None),
        P("fsdp", None, "sp", None),
        P("sp", None, None),
        P("sp", None, None),
    )
    out_specs = (P("fsdp", None, "sp", None), P("fsdp", "sp", None))
    shards = make_shards(mesh.shape["fsdp"], mesh.shape["sp"])
    return jax.shard_map(shards, mesh=mesh, in_specs=in_specs, out_specs=out_specs, check_vma=False)
```

profile of v0, /device:TPU:1, one launch (start us, length us, event | category | flops | bytes accessed | tf_op | source)
XLA Modules:
  0.0 137.5 jit_solution(10325817535522382967)
XLA Ops:
  2.2 2.1 %collective-permute-start.1 = (bf16[192,1536]{1,0:T(8,128)(2,1)S(1)}, bf16[192,1536]{1,0:T(8,128)(2,1)S(1)}, u32[]{:S(2)}, u32[]{:S(2)}) collective-permute-start(bf16[192,1536]{1,0:T(8,128)(2,1)S(1)} %reshape.25.refs_0_), channel_id=1, source_target_pairs={{0,16},{4,20},{8,24},{12,28},{16,0},{20,4},{24,8},{28,12},{1,17},{... | collective-permute-start | bytes 1769480 | tf_op jit(solution)/shard_map/ppermute | solution.py:241
  6.7 2.4 %collective-permute-start.8 = (bf16[128,1536]{1,0:T(8,128)(2,1)S(1)}, bf16[128,1536]{1,0:T(8,128)(2,1)S(1)}, u32[]{:S(2)}, u32[]{:S(2)}) collective-permute-start(bf16[128,1536]{1,0:T(8,128)(2,1)S(1)} %get-tuple-element.25), channel_id=1, source_target_pairs={{0,2},{2,3},{3,1},{1,0},{4,6},{6,7},{7,5},{5,4},{8,10},{10,11},{11... | collective-permute-start | bytes 1179656 | tf_op jit(solution)/shard_map/ppermute | solution.py:280
  10.4 7.1 %collective-permute-done.1.refs_2_ = bf16[192,1536]{1,0:T(8,128)(2,1)S(1)} collective-permute-done((bf16[192,1536]{1,0:T(8,128)(2,1)S(1)}, bf16[192,1536]{1,0:T(8,128)(2,1)S(1)}, u32[]{:S(2)}, u32[]{:S(2)}) %collective-permute-start.1) | collective-permute-done | bytes 589856 | tf_op jit(solution)/shard_map/ppermute | solution.py:241
  18.7 1.7 %collective-permute-start.4 = (bf16[192,1536]{1,0:T(8,128)(2,1)S(1)}, bf16[192,1536]{1,0:T(8,128)(2,1)S(1)}, u32[]{:S(2)}, u32[]{:S(2)}) collective-permute-start(bf16[192,1536]{1,0:T(8,128)(2,1)S(1)} %reshape.25.refs_0_), channel_id=1, source_target_pairs={{0,4},{4,0},{8,12},{12,8},{16,20},{20,16},{24,28},{28,24},{1,5},{5... | collective-permute-start | bytes 1769480 | tf_op jit(solution)/shard_map/ppermute | solution.py:241
  22.7 2.3 %collective-permute-start.10 = (bf16[128,1536]{1,0:T(8,128)(2,1)S(1)}, bf16[128,1536]{1,0:T(8,128)(2,1)}, u32[]{:S(2)}, u32[]{:S(2)}) collective-permute-start(bf16[128,1536]{1,0:T(8,128)(2,1)S(1)} %collective-permute-done.8.refs_9_), channel_id=1, source_target_pairs={{0,2},{2,3},{3,1},{1,0},{4,6},{6,7},{7,5},{5,4},{8,10},{10,11},{11... | collective-permute-start | bytes 1179656 | tf_op jit(solution)/shard_map/ppermute | solution.py:280
  25.0 2.8 %collective-permute-start.11 = (bf16[128,1536]{1,0:T(8,128)(2,1)S(1)}, bf16[128,1536]{1,0:T(8,128)(2,1)}, u32[]{:S(2)}, u32[]{:S(2)}) collective-permute-start(bf16[128,1536]{1,0:T(8,128)(2,1)S(1)} %collective-permute-done.9.refs_10_), channel_id=1, source_target_pairs={{0,2},{2,3},{3,1},{1,0},{4,6},{6,7},{7,5},{5,4},{8,10},{10,11},{11... | collective-permute-start | bytes 1179656 | tf_op jit(solution)/shard_map/ppermute | solution.py:280
  27.8 3.3 %collective-permute-start.5 = (bf16[192,1536]{1,0:T(8,128)(2,1)}, bf16[192,1536]{1,0:T(8,128)(2,1)}, u32[]{:S(2)}, u32[]{:S(2)}) collective-permute-start(bf16[192,1536]{1,0:T(8,128)(2,1)} %collective-permute-done.refs_1_), channel_id=1, source_target_pairs={{0,4},{4,0},{8,12},{12,8},{16,20},{20,16},{24,28},{28,24},{1,5},{5... | collective-permute-start | bytes 1769480 | tf_op jit(solution)/shard_map/ppermute | solution.py:241
  34.8 2.4 %collective-permute-start.12 = (bf16[128,1536]{1,0:T(8,128)(2,1)}, bf16[128,1536]{1,0:T(8,128)(2,1)}, u32[]{:S(2)}, u32[]{:S(2)}) collective-permute-start(bf16[128,1536]{1,0:T(8,128)(2,1)} %collective-permute-done.10.refs_11_), channel_id=1, source_target_pairs={{0,2},{2,3},{3,1},{1,0},{4,6},{6,7},{7,5},{5,4},{8,10},{10,11},{11... | collective-permute-start | bytes 1179656 | tf_op jit(solution)/shard_map/ppermute | solution.py:280
  37.2 5.2 %collective-permute-done.11.refs_12_ = bf16[128,1536]{1,0:T(8,128)(2,1)} collective-permute-done((bf16[128,1536]{1,0:T(8,128)(2,1)S(1)}, bf16[128,1536]{1,0:T(8,128)(2,1)}, u32[]{:S(2)}, u32[]{:S(2)}) %collective-permute-start.11) | collective-permute-done | bytes 393248 | tf_op jit(solution)/shard_map/ppermute | solution.py:280
  42.4 3.2 %collective-permute-start.13 = (bf16[128,1536]{1,0:T(8,128)(2,1)}, bf16[128,1536]{1,0:T(8,128)(2,1)}, u32[]{:S(2)}, u32[]{:S(2)}) collective-permute-start(bf16[128,1536]{1,0:T(8,128)(2,1)} %collective-permute-done.11.refs_12_), channel_id=1, source_target_pairs={{0,2},{2,3},{3,1},{1,0},{4,6},{6,7},{7,5},{5,4},{8,10},{10,11},{11... | collective-permute-start | bytes 1179656 | tf_op jit(solution)/shard_map/ppermute | solution.py:280
  49.6 7.7 %project.1 = (bf16[1536,1536]{1,0:T(8,128)(2,1)S(1)}, bf16[768,1536]{1,0:T(8,128)(2,1)S(1)}) custom-call(s32[8]{0:T(128)S(1)} %broadcast_xor_fusion.owner_ref, bf16[192,1536]{1,0:T(8,128)(2,1)S(1)} %reshape.25.refs_0_, bf16[192,1536]{1,0:T(8,128)(2,1)} %collective-permute-done.refs_1_, bf16[192,1536]{1,0:T(8,128)(2,1)S(1)} %collective-permute-done.1.refs_2_, ...), custom_call_target="tpu_custom_call" | custom-call | flops 3623878656 | bytes 14155776 | tf_op jit(solution)/shard_map/project/pallas_call | solution.py:52
  57.3 2.0 %collective-permute-done.13.last_ref = bf16[128,1536]{1,0:T(8,128)(2,1)} collective-permute-done((bf16[128,1536]{1,0:T(8,128)(2,1)}, bf16[128,1536]{1,0:T(8,128)(2,1)}, u32[]{:S(2)}, u32[]{:S(2)}) %collective-permute-start.13) | collective-permute-done | bytes 393248 | tf_op jit(solution)/shard_map/ppermute | solution.py:280
  59.3 24.6 %attention.1 = (bf16[1024,512]{1,0:T(8,128)(2,1)S(1)}, bf16[1024,1536]{1,0:T(8,128)(2,1)S(1)}, bf16[128,1536]{1,0:T(8,128)(2,1)S(1)}, bf16[128,1536]{1,0:T(8,128)(2,1)S(1)}) custom-call(s32[8]{0:T(128)S(1)} %fusion.place_ref, s32[128]{0:T(128)S(1)} %reshape.23.tiles_ref, s32[128]{0:T(128)S(1)} %reshape.24.live_ref, ...), custom_call_target="tpu_custom_call" | custom-call | flops 3221225472 | bytes 8388608 | tf_op jit(solution)/shard_map/attention/pallas_call | solution.py:201
  83.9 3.1 %collective-permute-start.17 = (bf16[128,1536]{1,0:T(8,128)(2,1)S(1)}, bf16[128,1536]{1,0:T(8,128)(2,1)S(1)}, u32[]{:S(2)}, u32[]{:S(2)}) collective-permute-start(bf16[128,1536]{1,0:T(8,128)(2,1)S(1)} %get-tuple-element.23), channel_id=1, source_target_pairs={{0,2},{2,3},{3,1},{1,0},{4,6},{6,7},{7,5},{5,4},{8,10},{10,11},{11... | collective-permute-start | bytes 1179656 | tf_op jit(solution)/shard_map/ppermute | solution.py:298
  87.5 7.3 %products.1 = (f32[128,1536]{1,0:T(8,128)S(1)}, f32[128,1536]{1,0:T(8,128)S(1)}, f32[128,1536]{1,0:T(8,128)S(1)}, f32[128,1536]{1,0:T(8,128)S(1)}, f32[256,1536]{1,0:T(8,128)S(1)}) custom-call(bf16[1024,1536]{1,0:T(8,128)(2,1)S(1)} %get-tuple-element.16.dqkv_ref, bf16[1536,1536]{1,0:T(8,128)(2,1)S(1)} %get-tuple-element.14.w_ref), custom_call_target="tpu_custom_call" | custom-call | flops 3623878656 | bytes 11796480 | tf_op jit(solution)/shard_map/products/pallas_call | solution.py:84
  94.9 2.6 %collective-permute-start.18 = (bf16[128,1536]{1,0:T(8,128)(2,1)S(1)}, bf16[128,1536]{1,0:T(8,128)(2,1)S(1)}, u32[]{:S(2)}, u32[]{:S(2)}) collective-permute-start(bf16[128,1536]{1,0:T(8,128)(2,1)S(1)} %add_convert_fusion.1), channel_id=1, source_target_pairs={{0,2},{2,3},{3,1},{1,0},{4,6},{6,7},{7,5},{5,4},{8,10},{10,11},{11... | collective-permute-start | bytes 1179656 | tf_op jit(solution)/shard_map/ppermute | solution.py:298
  97.5 5.2 %collective-permute-done.14 = bf16[128,1536]{1,0:T(8,128)(2,1)S(1)} collective-permute-done((bf16[128,1536]{1,0:T(8,128)(2,1)S(1)}, bf16[128,1536]{1,0:T(8,128)(2,1)S(1)}, u32[]{:S(2)}, u32[]{:S(2)}) %collective-permute-start.14) | collective-permute-done | bytes 393248 | tf_op jit(solution)/shard_map/ppermute | solution.py:295
  102.8 3.1 %collective-permute-start.15 = (bf16[128,1536]{1,0:T(8,128)(2,1)S(1)}, bf16[128,1536]{1,0:T(8,128)(2,1)S(1)}, u32[]{:S(2)}, u32[]{:S(2)}) collective-permute-start(bf16[128,1536]{1,0:T(8,128)(2,1)S(1)} %add_convert_fusion.3), channel_id=1, source_target_pairs={{0,2},{2,3},{3,1},{1,0},{4,6},{6,7},{7,5},{5,4},{8,10},{10,11},{11... | collective-permute-start | bytes 1179656 | tf_op jit(solution)/shard_map/ppermute | solution.py:295
  105.9 5.2 %collective-permute-done.18 = bf16[128,1536]{1,0:T(8,128)(2,1)S(1)} collective-permute-done((bf16[128,1536]{1,0:T(8,128)(2,1)S(1)}, bf16[128,1536]{1,0:T(8,128)(2,1)S(1)}, u32[]{:S(2)}, u32[]{:S(2)}) %collective-permute-start.18) | collective-permute-done | bytes 393248 | tf_op jit(solution)/shard_map/ppermute | solution.py:298
  112.0 3.1 %collective-permute-start.19 = (bf16[128,1536]{1,0:T(8,128)(2,1)}, bf16[128,1536]{1,0:T(8,128)(2,1)S(1)}, u32[]{:S(2)}, u32[]{:S(2)}) collective-permute-start(bf16[128,1536]{1,0:T(8,128)(2,1)} %add_convert_fusion), channel_id=1, source_target_pairs={{0,2},{2,3},{3,1},{1,0},{4,6},{6,7},{7,5},{5,4},{8,10},{10,11},{11... | collective-permute-start | bytes 1179656 | tf_op jit(solution)/shard_map/ppermute | solution.py:298
  115.0 4.5 %collective-permute-done.15 = bf16[128,1536]{1,0:T(8,128)(2,1)S(1)} collective-permute-done((bf16[128,1536]{1,0:T(8,128)(2,1)S(1)}, bf16[128,1536]{1,0:T(8,128)(2,1)S(1)}, u32[]{:S(2)}, u32[]{:S(2)}) %collective-permute-start.15) | collective-permute-done | bytes 393248 | tf_op jit(solution)/shard_map/ppermute | solution.py:295
  120.4 3.1 %collective-permute-start.16 = (bf16[128,1536]{1,0:T(8,128)(2,1)}, bf16[128,1536]{1,0:T(8,128)(2,1)S(1)}, u32[]{:S(2)}, u32[]{:S(2)}) collective-permute-start(bf16[128,1536]{1,0:T(8,128)(2,1)} %add_convert_fusion.2), channel_id=1, source_target_pairs={{0,2},{2,3},{3,1},{1,0},{4,6},{6,7},{7,5},{5,4},{8,10},{10,11},{11... | collective-permute-start | bytes 1179656 | tf_op jit(solution)/shard_map/ppermute | solution.py:295
  124.5 3.5 %collective-permute-done.19.high_ref = bf16[128,1536]{1,0:T(8,128)(2,1)S(1)} collective-permute-done((bf16[128,1536]{1,0:T(8,128)(2,1)}, bf16[128,1536]{1,0:T(8,128)(2,1)S(1)}, u32[]{:S(2)}, u32[]{:S(2)}) %collective-permute-start.19) | collective-permute-done | bytes 393248 | tf_op jit(solution)/shard_map/ppermute | solution.py:298
  128.1 8.4 %collective-permute-done.16.low_ref = bf16[128,1536]{1,0:T(8,128)(2,1)S(1)} collective-permute-done((bf16[128,1536]{1,0:T(8,128)(2,1)}, bf16[128,1536]{1,0:T(8,128)(2,1)S(1)}, u32[]{:S(2)}, u32[]{:S(2)}) %collective-permute-start.16) | collective-permute-done | bytes 393248 | tf_op jit(solution)/shard_map/ppermute | solution.py:295
  (57 shorter events, 20.7 us)
Async XLA Ops:
  0.6 45.0 %copy-start.7 = (s32[8]{0:T(128)S(1)}, s32[8]{0:T(128)}, u32[]{:S(2)}) copy-start(s32[8]{0:T(128)} %constant.33.clone) | copy-start | bytes 100
  2.2 44.8 %copy-start.5 = (s32[4,8,4]{1,2,0:T(4,128)S(1)}, s32[4,8,4]{1,2,0:T(4,128)}, u32[]{:S(2)}) copy-start(s32[4,8,4]{1,2,0:T(4,128)} %param.10) | copy-start | bytes 1540
  2.2 45.0 %copy-start.6 = (s32[4,8,4]{1,2,0:T(4,128)S(1)}, s32[4,8,4]{1,2,0:T(4,128)}, u32[]{:S(2)}) copy-start(s32[4,8,4]{1,2,0:T(4,128)} %param.11) | copy-start | bytes 1540
  2.2 45.3 %copy-start = (bf16[1,256,1536]{2,1,0:T(8,128)(2,1)S(1)}, bf16[1,256,1536]{2,1,0:T(8,128)(2,1)}, u32[]{:S(2)}) copy-start(bf16[1,256,1536]{2,1,0:T(8,128)(2,1)} %param.7) | copy-start | bytes 2359300
  2.2 15.3 %collective-permute-start.1 = (bf16[192,1536]{1,0:T(8,128)(2,1)S(1)}, bf16[192,1536]{1,0:T(8,128)(2,1)S(1)}, u32[]{:S(2)}, u32[]{:S(2)}) collective-permute-start(bf16[192,1536]{1,0:T(8,128)(2,1)S(1)} %reshape.25.refs_0_), channel_id=1, source_target_pairs={{0,16},{4,20},{8,24},{12,28},{16,0},{20,4},{24,8},{28,12},{1,17},{... | collective-permute-start | bytes 1769480 | tf_op jit(solution)/shard_map/ppermute | solution.py:241
  4.3 16.1 %collective-permute-start = (bf16[192,1536]{1,0:T(8,128)(2,1)S(1)}, bf16[192,1536]{1,0:T(8,128)(2,1)}, u32[]{:S(2)}, u32[]{:S(2)}) collective-permute-start(bf16[192,1536]{1,0:T(8,128)(2,1)S(1)} %reshape.25.refs_0_), channel_id=1, source_target_pairs={{0,8},{4,12},{8,0},{12,4},{16,24},{20,28},{24,16},{28,20},{1,9},{5... | collective-permute-start | bytes 1769480 | tf_op jit(solution)/shard_map/ppermute | solution.py:241
  6.7 16.0 %collective-permute-start.8 = (bf16[128,1536]{1,0:T(8,128)(2,1)S(1)}, bf16[128,1536]{1,0:T(8,128)(2,1)S(1)}, u32[]{:S(2)}, u32[]{:S(2)}) collective-permute-start(bf16[128,1536]{1,0:T(8,128)(2,1)S(1)} %get-tuple-element.25), channel_id=1, source_target_pairs={{0,2},{2,3},{3,1},{1,0},{4,6},{6,7},{7,5},{5,4},{8,10},{10,11},{11... | collective-permute-start | bytes 1179656 | tf_op jit(solution)/shard_map/ppermute | solution.py:280
  9.1 16.0 %collective-permute-start.9 = (bf16[128,1536]{1,0:T(8,128)(2,1)S(1)}, bf16[128,1536]{1,0:T(8,128)(2,1)S(1)}, u32[]{:S(2)}, u32[]{:S(2)}) collective-permute-start(bf16[128,1536]{1,0:T(8,128)(2,1)S(1)} %get-tuple-element.24), channel_id=1, source_target_pairs={{0,2},{2,3},{3,1},{1,0},{4,6},{6,7},{7,5},{5,4},{8,10},{10,11},{11... | collective-permute-start | bytes 1179656 | tf_op jit(solution)/shard_map/ppermute | solution.py:280
  17.5 10.3 %collective-permute-start.2 = (bf16[96,1536]{1,0:T(8,128)(2,1)S(1)}, bf16[96,1536]{1,0:T(8,128)(2,1)S(1)}, u32[]{:S(2)}, u32[]{:S(2)}) collective-permute-start(bf16[96,1536]{1,0:T(8,128)(2,1)S(1)} %slice.24), channel_id=1, source_target_pairs={{0,8},{4,12},{8,0},{12,4},{16,24},{20,28},{24,16},{28,20},{1,9},{5... | collective-permute-start | bytes 884744 | tf_op jit(solution)/shard_map/ppermute | solution.py:241
  18.7 13.9 %collective-permute-start.4 = (bf16[192,1536]{1,0:T(8,128)(2,1)S(1)}, bf16[192,1536]{1,0:T(8,128)(2,1)S(1)}, u32[]{:S(2)}, u32[]{:S(2)}) collective-permute-start(bf16[192,1536]{1,0:T(8,128)(2,1)S(1)} %reshape.25.refs_0_), channel_id=1, source_target_pairs={{0,4},{4,0},{8,12},{12,8},{16,20},{20,16},{24,28},{28,24},{1,5},{5... | collective-permute-start | bytes 1769480 | tf_op jit(solution)/shard_map/ppermute | solution.py:241
  21.4 10.4 %collective-permute-start.3 = (bf16[96,1536]{1,0:T(8,128)(2,1)S(1)}, bf16[96,1536]{1,0:T(8,128)(2,1)S(1)}, u32[]{:S(2)}, u32[]{:S(2)}) collective-permute-start(bf16[96,1536]{1,0:T(8,128)(2,1)S(1)} %slice.25), channel_id=1, source_target_pairs={{0,16},{4,20},{8,24},{12,28},{16,0},{20,4},{24,8},{28,12},{1,17},{... | collective-permute-start | bytes 884744 | tf_op jit(solution)/shard_map/ppermute | solution.py:241
  22.7 12.1 %collective-permute-start.10 = (bf16[128,1536]{1,0:T(8,128)(2,1)S(1)}, bf16[128,1536]{1,0:T(8,128)(2,1)}, u32[]{:S(2)}, u32[]{:S(2)}) collective-permute-start(bf16[128,1536]{1,0:T(8,128)(2,1)S(1)} %collective-permute-done.8.refs_9_), channel_id=1, source_target_pairs={{0,2},{2,3},{3,1},{1,0},{4,6},{6,7},{7,5},{5,4},{8,10},{10,11},{11... | collective-permute-start | bytes 1179656 | tf_op jit(solution)/shard_map/ppermute | solution.py:280
  25.0 17.4 %collective-permute-start.11 = (bf16[128,1536]{1,0:T(8,128)(2,1)S(1)}, bf16[128,1536]{1,0:T(8,128)(2,1)}, u32[]{:S(2)}, u32[]{:S(2)}) collective-permute-start(bf16[128,1536]{1,0:T(8,128)(2,1)S(1)} %collective-permute-done.9.refs_10_), channel_id=1, source_target_pairs={{0,2},{2,3},{3,1},{1,0},{4,6},{6,7},{7,5},{5,4},{8,10},{10,11},{11... | collective-permute-start | bytes 1179656 | tf_op jit(solution)/shard_map/ppermute | solution.py:280
  27.8 19.6 %collective-permute-start.5 = (bf16[192,1536]{1,0:T(8,128)(2,1)}, bf16[192,1536]{1,0:T(8,128)(2,1)}, u32[]{:S(2)}, u32[]{:S(2)}) collective-permute-start(bf16[192,1536]{1,0:T(8,128)(2,1)} %collective-permute-done.refs_1_), channel_id=1, source_target_pairs={{0,4},{4,0},{8,12},{12,8},{16,20},{20,16},{24,28},{28,24},{1,5},{5... | collective-permute-start | bytes 1769480 | tf_op jit(solution)/shard_map/ppermute | solution.py:241
  31.9 15.6 %collective-permute-start.6 = (bf16[192,1536]{1,0:T(8,128)(2,1)S(1)}, bf16[192,1536]{1,0:T(8,128)(2,1)}, u32[]{:S(2)}, u32[]{:S(2)}) collective-permute-start(bf16[192,1536]{1,0:T(8,128)(2,1)S(1)} %collective-permute-done.1.refs_2_), channel_id=1, source_target_pairs={{0,4},{4,0},{8,12},{12,8},{16,20},{20,16},{24,28},{28,24},{1,5},{5... | collective-permute-start | bytes 1769480 | tf_op jit(solution)/shard_map/ppermute | solution.py:241
  33.4 14.1 %collective-permute-start.7 = (bf16[192,1536]{1,0:T(8,128)(2,1)}, bf16[192,1536]{1,0:T(8,128)(2,1)}, u32[]{:S(2)}, u32[]{:S(2)}) collective-permute-start(bf16[192,1536]{1,0:T(8,128)(2,1)} %constant_dynamic-update-slice_fusion.refs_3_), channel_id=1, source_target_pairs={{0,4},{4,0},{8,12},{12,8},{16,20},{20,16},{24,28},{28,24},{1,5},{5... | collective-permute-start | bytes 1769480 | tf_op jit(solution)/shard_map/ppermute | solution.py:241
  34.8 22.5 %collective-permute-start.12 = (bf16[128,1536]{1,0:T(8,128)(2,1)}, bf16[128,1536]{1,0:T(8,128)(2,1)}, u32[]{:S(2)}, u32[]{:S(2)}) collective-permute-start(bf16[128,1536]{1,0:T(8,128)(2,1)} %collective-permute-done.10.refs_11_), channel_id=1, source_target_pairs={{0,2},{2,3},{3,1},{1,0},{4,6},{6,7},{7,5},{5,4},{8,10},{10,11},{11... | collective-permute-start | bytes 1179656 | tf_op jit(solution)/shard_map/ppermute | solution.py:280
  42.4 17.0 %collective-permute-start.13 = (bf16[128,1536]{1,0:T(8,128)(2,1)}, bf16[128,1536]{1,0:T(8,128)(2,1)}, u32[]{:S(2)}, u32[]{:S(2)}) collective-permute-start(bf16[128,1536]{1,0:T(8,128)(2,1)} %collective-permute-done.11.refs_12_), channel_id=1, source_target_pairs={{0,2},{2,3},{3,1},{1,0},{4,6},{6,7},{7,5},{5,4},{8,10},{10,11},{11... | collective-permute-start | bytes 1179656 | tf_op jit(solution)/shard_map/ppermute | solution.py:280
  83.9 10.9 %collective-permute-start.17 = (bf16[128,1536]{1,0:T(8,128)(2,1)S(1)}, bf16[128,1536]{1,0:T(8,128)(2,1)S(1)}, u32[]{:S(2)}, u32[]{:S(2)}) collective-permute-start(bf16[128,1536]{1,0:T(8,128)(2,1)S(1)} %get-tuple-element.23), channel_id=1, source_target_pairs={{0,2},{2,3},{3,1},{1,0},{4,6},{6,7},{7,5},{5,4},{8,10},{10,11},{11... | collective-permute-start | bytes 1179656 | tf_op jit(solution)/shard_map/ppermute | solution.py:298
  87.1 15.6 %collective-permute-start.14 = (bf16[128,1536]{1,0:T(8,128)(2,1)S(1)}, bf16[128,1536]{1,0:T(8,128)(2,1)S(1)}, u32[]{:S(2)}, u32[]{:S(2)}) collective-permute-start(bf16[128,1536]{1,0:T(8,128)(2,1)S(1)} %get-tuple-element.20), channel_id=1, source_target_pairs={{0,2},{2,3},{3,1},{1,0},{4,6},{6,7},{7,5},{5,4},{8,10},{10,11},{11... | collective-permute-start | bytes 1179656 | tf_op jit(solution)/shard_map/ppermute | solution.py:295
  94.9 16.2 %collective-permute-start.18 = (bf16[128,1536]{1,0:T(8,128)(2,1)S(1)}, bf16[128,1536]{1,0:T(8,128)(2,1)S(1)}, u32[]{:S(2)}, u32[]{:S(2)}) collective-permute-start(bf16[128,1536]{1,0:T(8,128)(2,1)S(1)} %add_convert_fusion.1), channel_id=1, source_target_pairs={{0,2},{2,3},{3,1},{1,0},{4,6},{6,7},{7,5},{5,4},{8,10},{10,11},{11... | collective-permute-start | bytes 1179656 | tf_op jit(solution)/shard_map/ppermute | solution.py:298
  102.8 16.8 %collective-permute-start.15 = (bf16[128,1536]{1,0:T(8,128)(2,1)S(1)}, bf16[128,1536]{1,0:T(8,128)(2,1)S(1)}, u32[]{:S(2)}, u32[]{:S(2)}) collective-permute-start(bf16[128,1536]{1,0:T(8,128)(2,1)S(1)} %add_convert_fusion.3), channel_id=1, source_target_pairs={{0,2},{2,3},{3,1},{1,0},{4,6},{6,7},{7,5},{5,4},{8,10},{10,11},{11... | collective-permute-start | bytes 1179656 | tf_op jit(solution)/shard_map/ppermute | solution.py:295
  112.0 16.1 %collective-permute-start.19 = (bf16[128,1536]{1,0:T(8,128)(2,1)}, bf16[128,1536]{1,0:T(8,128)(2,1)S(1)}, u32[]{:S(2)}, u32[]{:S(2)}) collective-permute-start(bf16[128,1536]{1,0:T(8,128)(2,1)} %add_convert_fusion), channel_id=1, source_target_pairs={{0,2},{2,3},{3,1},{1,0},{4,6},{6,7},{7,5},{5,4},{8,10},{10,11},{11... | collective-permute-start | bytes 1179656 | tf_op jit(solution)/shard_map/ppermute | solution.py:298
  120.4 16.1 %collective-permute-start.16 = (bf16[128,1536]{1,0:T(8,128)(2,1)}, bf16[128,1536]{1,0:T(8,128)(2,1)S(1)}, u32[]{:S(2)}, u32[]{:S(2)}) collective-permute-start(bf16[128,1536]{1,0:T(8,128)(2,1)} %add_convert_fusion.2), channel_id=1, source_target_pairs={{0,2},{2,3},{3,1},{1,0},{4,6},{6,7},{7,5},{5,4},{8,10},{10,11},{11... | collective-permute-start | bytes 1179656 | tf_op jit(solution)/shard_map/ppermute | solution.py:295
  (4 other events, 23.4 us)
where the time goes:
time: 140 us; the launch traced here: 137 us
  waiting for transfers between devices  41.3 us (30%)
  starting transfers between devices  41.1 us (29%)
  Pallas kernels  40.6 us (29%)
  local copies, waits for them, and re-layouts  11.1 us (8%)
  other arithmetic  2.52 us (2%)
    pallas_call x1, Pallas kernels, attention(): pl.pallas_call(functools.partial(attention_kernel, heads=heads, slots=slo...  24.6 us
    ppermute x3, waiting for transfers between devices, layer(): low = lax.ppermute(low, 'sp', ring)  18.2 us
    ppermute x6, starting transfers between devices, layer(): halves[side] = lax.ppermute(halves[side], 'sp', ring)  14.4 us
    ppermute x8, starting transfers between devices, swap(): return lax.ppermute(value, axis, [(i, i ^ bit) for i in range(count)])  11.3 us
    ppermute x3, starting transfers between devices, layer(): high = lax.ppermute(high, 'sp', ring)  8.77 us
    ppermute x3, waiting for transfers between devices, layer(): high = lax.ppermute(high, 'sp', ring)  8.76 us
    pallas_call x1, Pallas kernels, project(): pl.pallas_call(functools.partial(project_kernel, shards=len(shards), part...  7.74 us
    pallas_call x1, Pallas kernels, products(): pl.pallas_call(functools.partial(product_kernel, start=start), out_shape=...  7.29 us
  transfers between devices with their start and end apart: 20, of which 8 were waited for; matrix products, arithmetic and copies ran while one was open for 7% of the time, Pallas kernels for 11%

commit v1 on v0

v1 whole, which is shorter than its diff:
```python
import functools

import jax
import jax.numpy as jnp
from jax import lax
from jax.experimental import pallas as pl
from jax.experimental.pallas import tpu as pltpu
from jax.sharding import PartitionSpec as P


HEAD = 128
TILE = 128
NN = (((1,), (0,)), ((), ()))
NT = (((1,), (1,)), ((), ()))


PAUSE = 4400
LOG2E = 1.4426950408889634


def dot(a, b, dims):
    return lax.dot_general(a, b, dims, preferred_element_type=jnp.float32)


def weave(*streams):
    streams = [stream for stream in streams if stream is not None]
    while streams:
        streams = [stream for stream in streams if next(stream, None) is not None]


def project_kernel(*refs, keys, parts):
    shards = len(keys)
    mine = lax.axis_index("fsdp")
    shard_refs, part_refs = refs[:shards], refs[shards : shards + parts]
    w_ref, qkv_ref, sems = refs[shards + parts :]
    rows = shard_refs[0].shape[0]
    copies = []
    for number, shard in enumerate(shard_refs):
        at = pl.ds(pl.multiple_of((mine ^ keys[number]) * rows, rows), rows)
        copies.append(pltpu.make_async_copy(shard, w_ref.at[at], sems.at[number]))
    for copy in copies:
        copy.start()
    for copy in copies:
        copy.wait()
    start = 0
    for part in part_refs:
        size = part.shape[0]
        qkv_ref[start : start + size, :] = dot(part[...], w_ref[...], NN).astype(jnp.bfloat16)
        start += size


def project(keys, shards, parts):
    _, width = shards[0].shape
    depth = parts[0].shape[1]
    length = sum(part.shape[0] for part in parts)
    anywhere = pl.BlockSpec(memory_space=pl.ANY)
    return pl.pallas_call(
        functools.partial(project_kernel, keys=tuple(keys), parts=len(parts)),
        out_shape=(
            jax.ShapeDtypeStruct((depth, width), jnp.bfloat16),
            jax.ShapeDtypeStruct((length, width), jnp.bfloat16),
        ),
        in_specs=[anywhere] * len(shards) + [pl.BlockSpec(memory_space=pltpu.VMEM)] * len(parts),
        out_specs=(pl.BlockSpec(memory_space=pltpu.VMEM),) * 2,
        scratch_shapes=[pltpu.SemaphoreType.DMA((len(shards),))],
        name="project",
        cost_estimate=pl.CostEstimate(
            flops=2 * length * depth * width,
            bytes_accessed=4 * depth * width + 4 * length * width,
            transcendentals=0,
        ),
        compiler_params=pltpu.CompilerParams(vmem_limit_bytes=16 << 20),
    )(*shards, *parts)


def product_kernel(dqkv_ref, w_ref, *out_refs, start):
    for out_ref in out_refs:
        rows = out_ref.shape[0]
        start = start % dqkv_ref.shape[0]
        out_ref[...] = dot(dqkv_ref[start : start + rows, :], w_ref[...], NT).astype(out_ref.dtype)
        start += rows


def products(dqkv, w, start, sizes, dtype=jnp.float32):
    depth, width = w.shape
    return pl.pallas_call(
        functools.partial(product_kernel, start=start),
        out_shape=tuple(jax.ShapeDtypeStruct((size, depth), dtype) for size in sizes),
        name="products",
        cost_estimate=pl.CostEstimate(
            flops=2 * sum(sizes) * depth * width,
            bytes_accessed=2 * depth * width + 6 * sum(sizes) * depth,
            transcendentals=0,
        ),
        compiler_params=pltpu.CompilerParams(vmem_limit_bytes=12 << 20),
    )(dqkv, w)


def finish_kernel(own_ref, low_ref, high_ref, out_ref):
    half = low_ref.shape[0]
    out_ref[:half, :] = (own_ref[:half, :] + low_ref[...].astype(jnp.float32)).astype(jnp.bfloat16)
    out_ref[half:, :] = (own_ref[half:, :] + high_ref[...].astype(jnp.float32)).astype(jnp.bfloat16)


def finish(own, low, high):
    return pl.pallas_call(
        finish_kernel,
        out_shape=jax.ShapeDtypeStruct(own.shape, jnp.bfloat16),
        name="finish",
        compiler_params=pltpu.CompilerParams(vmem_limit_bytes=8 << 20),
    )(own, low, high)


def attention_kernel(
    code_ref, early_ref, late_ref, last_ref, w_ref, dout_ref,
    out_ref, dqkv_ref, first_ref, place_ref, qkv_ref, kt_ref, vt_ref, *refs,
    heads, slots, chunk,
):
    dkv_refs, score_refs, grad_refs, prob_refs, peak_refs = (
        refs[group * heads : (group + 1) * heads] for group in range(5)
    )
    sem = refs[5 * heads]
    length = qkv_ref.shape[0]
    width = heads * HEAD
    tile_count = length // TILE
    scale = HEAD ** (-0.5)
    per_chunk = chunk // TILE
    sp_count = length // chunk
    device = lax.axis_index("sp")
    spot = jnp.where(device % 2 == 0, device // 2, sp_count - 1 - device // 2)
    for number in range(sp_count):
        step = lax.rem(spot - ring_spot(number, sp_count) + sp_count, sp_count)
        for tile in range(per_chunk):
            place_ref[number * per_chunk + tile] = step * per_chunk + tile
    early = early_ref.shape[0]
    middle_row = early + late_ref.shape[0]
    copy = pltpu.make_async_copy(early_ref, qkv_ref.at[pl.ds(0, early)], sem)
    copy.start()
    qkv_ref[early:middle_row, :] = dot(late_ref[...], w_ref[...], NN).astype(jnp.bfloat16)
    qkv_ref[middle_row:, :] = dot(last_ref[...], w_ref[...], NN).astype(jnp.bfloat16)
    for head in range(heads):
        dkv_refs[head][...] = jnp.zeros_like(dkv_refs[head])
    copy.wait()
    for head in range(heads):
        at = head * HEAD
        kt_ref[head] = qkv_ref[:, width + at : width + at + HEAD].T
        vt_ref[head] = qkv_ref[:, 2 * width + at : 2 * width + at + HEAD].T

    def tile_rows(tile):
        return pl.ds(pl.multiple_of(tile * TILE, TILE), TILE)

    def spots_of(head, tile):
        base = (head * tile_count + tile) * slots
        return base, [tile_rows(place_ref[jnp.maximum(code_ref[base + s], 0)]) for s in range(slots)]

    def operands(head, tile):
        at = head * HEAD
        query = qkv_ref[tile_rows(place_ref[tile]), at : at + HEAD]
        return query, dout_ref[tile_rows(tile), at : at + HEAD]

    def enter(head, tile):
        at = head * HEAD
        base, spots = spots_of(head, tile)
        query, dout = operands(head, tile)
        peak = None
        empty = jnp.zeros((TILE, HEAD), jnp.bfloat16)
        both = jnp.concatenate([jnp.concatenate([query, empty], axis=1), jnp.concatenate([empty, dout], axis=1)], axis=0)
        for s in range(slots):
            key = qkv_ref[spots[s], width + at : width + at + HEAD]
            value = qkv_ref[spots[s], 2 * width + at : 2 * width + at + HEAD]
            part = dot(jnp.concatenate([key, value], axis=1), both, NT)
            score = part[:, :TILE]
            if s > 0:
                score = jnp.where(code_ref[base + s] >= 0, score, -1e30)
            score_refs[head][s * TILE : (s + 1) * TILE, :] = score
            grad_refs[head][s * TILE : (s + 1) * TILE, :] = part[:, TILE:]
            peak = score if peak is None else jnp.maximum(peak, score)
            yield True
            yield True
        peak_refs[head][...] = jnp.broadcast_to(jnp.max(peak, axis=0, keepdims=True), (8, TILE))

    def middle(head, tile):
        peak = peak_refs[head][:1, :]
        total = jnp.zeros((1, TILE), jnp.float32)
        delta = jnp.zeros((1, TILE), jnp.float32)
        for s in range(slots):
            part = slice(s * TILE, (s + 1) * TILE)
            grown = jnp.exp2((score_refs[head][part, :] - peak) * (scale * LOG2E))
            score_refs[head][part, :] = grown
            total += jnp.sum(grown, axis=0, keepdims=True)
            delta += jnp.sum(grown * grad_refs[head][part, :], axis=0, keepdims=True)
            yield True
        inverse = 1.0 / total
        delta = delta * inverse
        for s in range(slots):
            part = slice(s * TILE, (s + 1) * TILE)
            prob = score_refs[head][part, :] * inverse
            prob_refs[head][part, TILE:] = prob.astype(jnp.bfloat16)
            prob_refs[head][part, :TILE] = (prob * (grad_refs[head][part, :] - delta) * scale).astype(jnp.bfloat16)
            yield True

    def leave(head, tile):
        at = head * HEAD
        rows = tile_rows(tile)
        held = tile_rows(place_ref[tile])
        _, spots = spots_of(head, tile)
        query, dout = operands(head, tile)
        empty = jnp.zeros((TILE, HEAD), jnp.bfloat16)
        both = jnp.concatenate([jnp.concatenate([query, empty], axis=1), jnp.concatenate([empty, dout], axis=1)], axis=0)
        value_t = jnp.concatenate([vt_ref[head, :, spot] for spot in spots], axis=1)
        out_ref[rows, at : at + HEAD] = dot(value_t, prob_refs[head][:, TILE:], NN).T.astype(jnp.bfloat16)
        yield True
        key_t = jnp.concatenate([kt_ref[head, :, spot] for spot in spots], axis=1)
        dqkv_ref[held, at : at + HEAD] = dot(key_t, prob_refs[head][:, :TILE], NN).T.astype(jnp.bfloat16)
        yield True
        for s in range(slots):
            part = slice(s * TILE, (s + 1) * TILE)
            dkv_refs[head][spots[s], :] += dot(prob_refs[head][part, :], both, NN)
            yield True

    def before(head, tile, back):
        order = head - back
        return (order % heads, tile + order // heads)

    def turn(tile, first):
        for head in range(heads):
            weave(
                enter(head, tile),
                middle(*before(head, tile, 1)) if not first or head >= 1 else None,
                leave(*before(head, tile, 2)) if not first or head >= 2 else None,
            )

    turn(0, True)

    def step(tile, carry):
        turn(tile, False)
        return carry

    lax.fori_loop(1, tile_count, step, 0)
    weave(middle(heads - 1, tile_count - 1), leave(*before(heads, tile_count - 1, 2)))
    weave(leave(heads - 1, tile_count - 1))
    for head in range(heads):
        at = head * HEAD
        dqkv_ref[:, width + at : width + at + HEAD] = dkv_refs[head][:, :HEAD].astype(jnp.bfloat16)
        dqkv_ref[:, 2 * width + at : 2 * width + at + HEAD] = dkv_refs[head][:, HEAD:].astype(jnp.bfloat16)
    half = chunk // 2
    first_ref[...] = dot(dqkv_ref[chunk : chunk + half, :], w_ref[...], NT).astype(jnp.bfloat16)


def attention(early, late, last, w, dout, codes, chunk):
    length = dout.shape[0]
    heads, tile_count, slots = codes.shape
    width = heads * HEAD
    depth = w.shape[0]
    smem = pl.BlockSpec(memory_space=pltpu.SMEM)
    vmem = pl.BlockSpec(memory_space=pltpu.VMEM)
    anywhere = pl.BlockSpec(memory_space=pl.ANY)
    return pl.pallas_call(
        functools.partial(attention_kernel, heads=heads, slots=slots, chunk=chunk),
        out_shape=(
            jax.ShapeDtypeStruct((length, width), jnp.bfloat16),
            jax.ShapeDtypeStruct((length, 3 * width), jnp.bfloat16),
            jax.ShapeDtypeStruct((chunk // 2, depth), jnp.bfloat16),
        ),
        in_specs=[smem, anywhere, vmem, vmem, vmem, vmem],
        out_specs=(vmem, vmem, vmem),
        scratch_shapes=[
            pltpu.SMEM((tile_count,), jnp.int32),
            pltpu.VMEM((length, 3 * width), jnp.bfloat16),
            pltpu.VMEM((heads, HEAD, length), jnp.bfloat16),
            pltpu.VMEM((heads, HEAD, length), jnp.bfloat16),
        ]
        + [pltpu.VMEM((length, 2 * HEAD), jnp.float32)] * heads
        + [pltpu.VMEM((slots * TILE, TILE), jnp.float32)] * (2 * heads)
        + [pltpu.VMEM((slots * TILE, 2 * TILE), jnp.bfloat16)] * heads
        + [pltpu.VMEM((8, TILE), jnp.float32)] * heads
        + [pltpu.SemaphoreType.DMA],
        name="attention",
        cost_estimate=pl.CostEstimate(
            flops=12 * heads * tile_count * slots * TILE * TILE * HEAD,
            bytes_accessed=16 * length * width,
            transcendentals=heads * tile_count * slots * TILE * TILE,
        ),
        compiler_params=pltpu.CompilerParams(vmem_limit_bytes=26 << 20),
    )(codes.reshape(-1), early, late, last, w, dout)


def stagger_kernel(out_ref):
    turns = (lax.axis_index("fsdp") % 2) * PAUSE
    out_ref[0] = lax.fori_loop(0, turns, lambda _, x: (x * 5 + 3) & 1023, turns)


def stagger():
    return pl.pallas_call(
        stagger_kernel,
        out_shape=jax.ShapeDtypeStruct((1,), jnp.int32),
        out_specs=pl.BlockSpec(memory_space=pltpu.SMEM),
        name="stagger",
        compiler_params=pltpu.CompilerParams(has_side_effects=True),
    )()


def ring_spot(device, count):
    return device // 2 if device % 2 == 0 else count - 1 - device // 2


def weight_bits(count):
    return [1 << b for b in range(1, count.bit_length() - 1)]


def gather_weights(w, axis, count):
    def swap(value, bit):
        return lax.ppermute(value, axis, [(i, i ^ bit) for i in range(count)])

    held = {0: w, 1: swap(w, 1)}
    bits = weight_bits(count)
    if len(bits) == 2:
        low, high = bits
        for k in range(2):
            held[low | k] = swap(held[k], low)
            held[high | k] = swap(held[k], high)
        held[low | high] = swap(held[high], low)
        held[low | high | 1] = swap(held[low | 1], high)
    else:
        for bit in bits:
            held.update({k | bit: swap(v, bit) for k, v in list(held.items())})
    return held


def make_shards(fsdp_count, sp_count):
    order = sorted(range(sp_count), key=lambda device: ring_spot(device, sp_count))
    ring = [(order[i], order[(i + 1) % sp_count]) for i in range(sp_count)]

    def layer(tokens_in, w_qkv, grad_attn, kv_tiles, tile_live):
        tokens = tokens_in[0]
        chunk, _ = tokens.shape
        half = chunk // 2
        heads, tile_count, _ = kv_tiles.shape
        length = tile_count * TILE
        width = heads * HEAD
        codes = jnp.where(tile_live > 0, kv_tiles, -1)
        dout = grad_attn[0].reshape(length, width)
        held = gather_weights(w_qkv.reshape(w_qkv.shape[0], -1), "fsdp", fsdp_count)
        halves = [tokens[:half], tokens[half:]]
        parts = [tokens]
        for _ in range(1, sp_count):
            for side in range(2):
                halves[side] = lax.ppermute(halves[side], "sp", ring)
                parts.append(halves[side])
        stagger()
        w, early = project(list(held), list(held.values()), parts[:-2])
        out, dqkv, low = attention(
            early, parts[-2], parts[-1], w, dout, codes, chunk
        )
        (high,) = products(dqkv, w, chunk + half, [half], jnp.bfloat16)
        sums = []
        for step in range(2, sp_count):
            sums += products(dqkv, w, step * chunk, [half, half])
        sums += products(dqkv, w, 0, [chunk])
        for step in range(1, sp_count):
            if step > 1:
                low = (sums[2 * step - 4] + low.astype(jnp.float32)).astype(jnp.bfloat16)
            low = lax.ppermute(low, "sp", ring)
            if step > 1:
                high = (sums[2 * step - 3] + high.astype(jnp.float32)).astype(jnp.bfloat16)
            high = lax.ppermute(high, "sp", ring)
        grad_tokens = finish(sums[-1], low, high)
        out = out.reshape(1, length, heads, HEAD)
        return out, grad_tokens[None]

    return layer


def solution(mesh):
    in_specs = (
        P("fsdp", "sp", None),
        P("fsdp", None, "sp", None),
        P("fsdp", None, "sp", None),
        P("sp", None, None),
        P("sp", None, None),
    )
    out_specs = (P("fsdp", None, "sp", None), P("fsdp", "sp", None))
    shards = make_shards(mesh.shape["fsdp"], mesh.shape["sp"])
    return jax.shard_map(shards, mesh=mesh, in_specs=in_specs, out_specs=out_specs, check_vma=False)
```

time: 140 us -> 148 us (1.057); the launches traced: 137 us -> 147 us
  Pallas kernels: 40.6 us -> 58.8 us
  starting transfers between devices: 41.1 us -> 30.1 us
  local copies, waits for them, and re-layouts: 11.1 us -> 12.9 us
    pallas_call x1 -> x2, Pallas kernels: 7.74 us -> 28.4 us  [the longest x1 21.2 us: stagger(): pl.pallas_call(stagger_kernel, out_shape=jax.ShapeDtypeStruct((1,), jnp.i...]
    ppermute x6, waiting for transfers between devices: 7.27 us -> 19.1 us  [layer(): halves[side] = lax.ppermute(halves[side], 'sp', ring)]
    ppermute x3, waiting for transfers between devices: 18.2 us -> 12.5 us  [layer(): low = lax.ppermute(low, 'sp', ring)]
    ppermute x3, starting transfers between devices: 8.77 us -> 3.22 us  [layer(): high = lax.ppermute(high, 'sp', ring)]
    pallas_call x1, Pallas kernels: 24.6 us -> 19.1 us  [attention(): pl.pallas_call(functools.partial(attention_kernel, heads=heads, slots=slo...]
    ppermute x8 -> x7, starting transfers between devices: 11.3 us -> 6.2 us  [swap(): return lax.ppermute(value, axis, [(i, i ^ bit) for i in range(count)])]
    ppermute x8 -> x7, waiting for transfers between devices: 7.12 us -> 4.26 us  [swap(): return lax.ppermute(value, axis, [(i, i ^ bit) for i in range(count)])]
    ppermute x3, waiting for transfers between devices: 8.76 us -> 6.53 us  [layer(): high = lax.ppermute(high, 'sp', ring)]
  transfers between devices with their start and end apart: 20 -> 19, of which waited for: 8 -> 9; matrix products, arithmetic and copies ran while one was open for 7% -> 7% of each run, Pallas kernels for 11% -> 24%
where the time goes in v1:
time: 148 us; the launch traced here: 147 us
  Pallas kernels  58.8 us (40%)
  waiting for transfers between devices  42.4 us (29%)
  starting transfers between devices  30.1 us (20%)
  local copies, waits for them, and re-layouts  12.9 us (9%)
  other arithmetic  2.48 us (2%)
    pallas_call x1, Pallas kernels, stagger(): pl.pallas_call(stagger_kernel, out_shape=jax.ShapeDtypeStruct((1,), jnp.i...  21.2 us
    pallas_call x1, Pallas kernels, attention(): pl.pallas_call(functools.partial(attention_kernel, heads=heads, slots=slo...  19.1 us
    ppermute x6, waiting for transfers between devices, layer(): halves[side] = lax.ppermute(halves[side], 'sp', ring)  19.1 us
    ppermute x6, starting transfers between devices, layer(): halves[side] = lax.ppermute(halves[side], 'sp', ring)  16.3 us
    ppermute x3, waiting for transfers between devices, layer(): low = lax.ppermute(low, 'sp', ring)  12.5 us
    pallas_call x4, Pallas kernels, products(): pl.pallas_call(functools.partial(product_kernel, start=start), out_shape=...  9.18 us
    pallas_call x1, Pallas kernels, project(): pl.pallas_call(functools.partial(project_kernel, keys=tuple(keys), parts=...  7.21 us
    ppermute x3, waiting for transfers between devices, layer(): high = lax.ppermute(high, 'sp', ring)  6.53 us
  transfers between devices with their start and end apart: 19, of which 9 were waited for; matrix products, arithmetic and copies ran while one was open for 7% of the time, Pallas kernels for 24%

profile of v1, /device:TPU:1, one launch (start us, length us, event | category | flops | bytes accessed | tf_op | source)
XLA Modules:
  0.0 147.4 jit_solution(4052181784554589986)
XLA Ops:
  2.3 2.7 %collective-permute-start.2 = (bf16[192,1536]{1,0:T(8,128)(2,1)S(1)}, bf16[192,1536]{1,0:T(8,128)(2,1)S(1)}, u32[]{:S(2)}, u32[]{:S(2)}) collective-permute-start(bf16[192,1536]{1,0:T(8,128)(2,1)S(1)} %reshape.16.refs_0_), channel_id=1, source_target_pairs={{0,16},{4,20},{8,24},{12,28},{16,0},{20,4},{24,8},{28,12},{1,17},{... | collective-permute-start | bytes 1769480 | tf_op jit(solution)/shard_map/ppermute | solution.py:313
  7.8 2.4 %collective-permute-start.7 = (bf16[128,1536]{1,0:T(8,128)(2,1)S(1)}, bf16[128,1536]{1,0:T(8,128)(2,1)S(1)}, u32[]{:S(2)}, u32[]{:S(2)}) collective-permute-start(bf16[128,1536]{1,0:T(8,128)(2,1)S(1)} %get-tuple-element.21), channel_id=1, source_target_pairs={{0,2},{2,3},{3,1},{1,0},{4,6},{6,7},{7,5},{5,4},{8,10},{10,11},{11... | collective-permute-start | bytes 1179656 | tf_op jit(solution)/shard_map/ppermute | solution.py:348
  11.5 6.4 %collective-permute-done.7.refs_9_ = bf16[128,1536]{1,0:T(8,128)(2,1)S(1)} collective-permute-done((bf16[128,1536]{1,0:T(8,128)(2,1)S(1)}, bf16[128,1536]{1,0:T(8,128)(2,1)S(1)}, u32[]{:S(2)}, u32[]{:S(2)}) %collective-permute-start.7) | collective-permute-done | bytes 393248 | tf_op jit(solution)/shard_map/ppermute | solution.py:348
  17.9 3.1 %collective-permute-start.9 = (bf16[128,1536]{1,0:T(8,128)(2,1)S(1)}, bf16[128,1536]{1,0:T(8,128)(2,1)}, u32[]{:S(2)}, u32[]{:S(2)}) collective-permute-start(bf16[128,1536]{1,0:T(8,128)(2,1)S(1)} %collective-permute-done.7.refs_9_), channel_id=1, source_target_pairs={{0,2},{2,3},{3,1},{1,0},{4,6},{6,7},{7,5},{5,4},{8,10},{10,11},{11... | collective-permute-start | bytes 1179656 | tf_op jit(solution)/shard_map/ppermute | solution.py:348
  21.0 5.3 %collective-permute-done.8.refs_10_ = bf16[128,1536]{1,0:T(8,128)(2,1)S(1)} collective-permute-done((bf16[128,1536]{1,0:T(8,128)(2,1)S(1)}, bf16[128,1536]{1,0:T(8,128)(2,1)S(1)}, u32[]{:S(2)}, u32[]{:S(2)}) %collective-permute-start.8) | collective-permute-done | bytes 393248 | tf_op jit(solution)/shard_map/ppermute | solution.py:348
  26.3 3.1 %collective-permute-start.10 = (bf16[128,1536]{1,0:T(8,128)(2,1)S(1)}, bf16[128,1536]{1,0:T(8,128)(2,1)}, u32[]{:S(2)}, u32[]{:S(2)}) collective-permute-start(bf16[128,1536]{1,0:T(8,128)(2,1)S(1)} %collective-permute-done.8.refs_10_), channel_id=1, source_target_pairs={{0,2},{2,3},{3,1},{1,0},{4,6},{6,7},{7,5},{5,4},{8,10},{10,11},{11... | collective-permute-start | bytes 1179656 | tf_op jit(solution)/shard_map/ppermute | solution.py:348
  32.6 2.2 %collective-permute-done.9.refs_11_ = bf16[128,1536]{1,0:T(8,128)(2,1)} collective-permute-done((bf16[128,1536]{1,0:T(8,128)(2,1)S(1)}, bf16[128,1536]{1,0:T(8,128)(2,1)}, u32[]{:S(2)}, u32[]{:S(2)}) %collective-permute-start.9) | collective-permute-done | bytes 393248 | tf_op jit(solution)/shard_map/ppermute | solution.py:348
  34.7 3.2 %collective-permute-start.11 = (bf16[128,1536]{1,0:T(8,128)(2,1)}, bf16[128,1536]{1,0:T(8,128)(2,1)}, u32[]{:S(2)}, u32[]{:S(2)}) collective-permute-start(bf16[128,1536]{1,0:T(8,128)(2,1)} %collective-permute-done.9.refs_11_), channel_id=1, source_target_pairs={{0,2},{2,3},{3,1},{1,0},{4,6},{6,7},{7,5},{5,4},{8,10},{10,11},{11... | collective-permute-start | bytes 1179656 | tf_op jit(solution)/shard_map/ppermute | solution.py:348
  37.9 5.2 %collective-permute-done.10.refs_12_ = bf16[128,1536]{1,0:T(8,128)(2,1)} collective-permute-done((bf16[128,1536]{1,0:T(8,128)(2,1)S(1)}, bf16[128,1536]{1,0:T(8,128)(2,1)}, u32[]{:S(2)}, u32[]{:S(2)}) %collective-permute-start.10) | collective-permute-done | bytes 393248 | tf_op jit(solution)/shard_map/ppermute | solution.py:348
  43.1 3.2 %collective-permute-start.12 = (bf16[128,1536]{1,0:T(8,128)(2,1)}, bf16[128,1536]{1,0:T(8,128)(2,1)}, u32[]{:S(2)}, u32[]{:S(2)}) collective-permute-start(bf16[128,1536]{1,0:T(8,128)(2,1)} %collective-permute-done.10.refs_12_), channel_id=1, source_target_pairs={{0,2},{2,3},{3,1},{1,0},{4,6},{6,7},{7,5},{5,4},{8,10},{10,11},{11... | collective-permute-start | bytes 1179656 | tf_op jit(solution)/shard_map/ppermute | solution.py:348
  47.1 2.4 %copy.11 = bf16[128,8,4,128]{3,1,2,0:T(8,128)(2,1)} copy(bf16[128,8,4,128]{3,2,1,0:T(4,128)(2,1)} %bitcast.13) | data formatting | bytes 2097152
  51.0 3.6 %collective-permute-done.6.refs_7_ = bf16[192,1536]{1,0:T(8,128)(2,1)} collective-permute-done((bf16[192,1536]{1,0:T(8,128)(2,1)}, bf16[192,1536]{1,0:T(8,128)(2,1)}, u32[]{:S(2)}, u32[]{:S(2)}) %collective-permute-start.6) | collective-permute-done | bytes 589856 | tf_op jit(solution)/shard_map/ppermute | solution.py:313
  55.6 7.2 %project.1 = (bf16[1536,1536]{1,0:T(8,128)(2,1)S(1)}, bf16[768,1536]{1,0:T(8,128)(2,1)S(1)}) custom-call(bf16[192,1536]{1,0:T(8,128)(2,1)S(1)} %reshape.16.refs_0_, bf16[192,1536]{1,0:T(8,128)(2,1)S(1)} %collective-permute-done.refs_1_, bf16[192,1536]{1,0:T(8,128)(2,1)S(1)} %collective-permute-done.1.refs_2_, ...), custom_call_target="tpu_custom_call" | custom-call | flops 3623878656 | bytes 14155776 | tf_op jit(solution)/shard_map/project/pallas_call | solution.py:57
  62.9 19.1 %attention.1 = (bf16[1024,512]{1,0:T(8,128)(2,1)S(1)}, bf16[1024,1536]{1,0:T(8,128)(2,1)S(1)}, bf16[128,1536]{1,0:T(8,128)(2,1)S(1)}) custom-call(s32[128]{0:T(128)S(1)} %reshape.15.code_ref, bf16[768,1536]{1,0:T(8,128)(2,1)S(1)} %get-tuple-element.11.early_ref, bf16[128,1536]{1,0:T(8,128)(2,1)} %collective-permute-done.11.late_ref, ...), custom_call_target="tpu_custom_call" | custom-call | flops 3221225472 | bytes 8388608 | tf_op jit(solution)/shard_map/attention/pallas_call | solution.py:258
  85.2 3.1 %products.6 = (f32[128,1536]{1,0:T(8,128)S(1)}, f32[128,1536]{1,0:T(8,128)S(1)}) custom-call(bf16[1024,1536]{1,0:T(8,128)(2,1)S(1)} %get-tuple-element.14.dqkv_ref, bf16[1536,1536]{1,0:T(8,128)(2,1)S(1)} %get-tuple-element.12.w_ref), custom_call_target="tpu_custom_call" | custom-call | flops 1207959552 | bytes 7077888 | tf_op jit(solution)/shard_map/products/pallas_call | solution.py:86
  88.3 3.1 %products.5 = (f32[128,1536]{1,0:T(8,128)S(1)}, f32[128,1536]{1,0:T(8,128)S(1)}) custom-call(bf16[1024,1536]{1,0:T(8,128)(2,1)S(1)} %get-tuple-element.14.dqkv_ref, bf16[1536,1536]{1,0:T(8,128)(2,1)S(1)} %get-tuple-element.12.w_ref), custom_call_target="tpu_custom_call" | custom-call | flops 1207959552 | bytes 7077888 | tf_op jit(solution)/shard_map/products/pallas_call | solution.py:86
  92.1 6.7 %collective-permute-done.13 = bf16[128,1536]{1,0:T(8,128)(2,1)S(1)} collective-permute-done((bf16[128,1536]{1,0:T(8,128)(2,1)S(1)}, bf16[128,1536]{1,0:T(8,128)(2,1)S(1)}, u32[]{:S(2)}, u32[]{:S(2)}) %collective-permute-start.13) | collective-permute-done | bytes 393248 | tf_op jit(solution)/shard_map/ppermute | solution.py:363
  98.9 1.8 %collective-permute-start.14 = (bf16[128,1536]{1,0:T(8,128)(2,1)S(1)}, bf16[128,1536]{1,0:T(8,128)(2,1)S(1)}, u32[]{:S(2)}, u32[]{:S(2)}) collective-permute-start(bf16[128,1536]{1,0:T(8,128)(2,1)S(1)} %add_convert_fusion.3), channel_id=1, source_target_pairs={{0,2},{2,3},{3,1},{1,0},{4,6},{6,7},{7,5},{5,4},{8,10},{10,11},{11... | collective-permute-start | bytes 1179656 | tf_op jit(solution)/shard_map/ppermute | solution.py:363
  100.7 6.5 %collective-permute-done.17 = bf16[128,1536]{1,0:T(8,128)(2,1)S(1)} collective-permute-done((bf16[128,1536]{1,0:T(8,128)(2,1)S(1)}, bf16[128,1536]{1,0:T(8,128)(2,1)S(1)}, u32[]{:S(2)}, u32[]{:S(2)}) %collective-permute-start.17) | collective-permute-done | bytes 393248 | tf_op jit(solution)/shard_map/ppermute | solution.py:366
  109.8 5.8 %collective-permute-done.14 = bf16[128,1536]{1,0:T(8,128)(2,1)S(1)} collective-permute-done((bf16[128,1536]{1,0:T(8,128)(2,1)S(1)}, bf16[128,1536]{1,0:T(8,128)(2,1)S(1)}, u32[]{:S(2)}, u32[]{:S(2)}) %collective-permute-start.14) | collective-permute-done | bytes 393248 | tf_op jit(solution)/shard_map/ppermute | solution.py:363
  118.2 21.2 %stagger.1 = s32[1]{0:T(128)} custom-call(), custom_call_target="tpu_custom_call" | custom-call | tf_op jit(solution)/shard_map/stagger/pallas_call | solution.py:294
  139.5 2.1 %reshape.17 = bf16[1,1024,4,128]{3,2,1,0:T(4,128)(2,1)} reshape(bf16[1024,512]{1,0:T(8,128)(2,1)} %copy-done.2) | data formatting | bytes 2097152 | tf_op jit(solution)/shard_map/reshape | solution.py:368
  141.6 2.3 %copy-done.1 = bf16[1536,1536]{1,0:T(8,128)(2,1)S(1)} copy-done((bf16[1536,1536]{1,0:T(8,128)(2,1)S(1)}, bf16[1536,1536]{1,0:T(8,128)(2,1)}, u32[]{:S(2)}) %copy-start.1) | copy-done | bytes 4718616
  145.4 2.0 %finish.1 = bf16[256,1536]{1,0:T(8,128)(2,1)} custom-call(f32[256,1536]{1,0:T(8,128)S(1)} %products.4.own_ref, bf16[128,1536]{1,0:T(8,128)(2,1)} %collective-permute-done.15.low_ref, bf16[128,1536]{1,0:T(8,128)(2,1)S(1)} %collective-permute-done.18.high_ref), custom_call_target="tpu_custom_call" | custom-call | tf_op jit(solution)/shard_map/finish/pallas_call | solution.py:106
  (47 shorter events, 22.7 us)
Async XLA Ops:
  0.6 54.0 %copy-start.4 = (bf16[1,256,1536]{2,1,0:T(8,128)(2,1)S(1)}, bf16[1,256,1536]{2,1,0:T(8,128)(2,1)}, u32[]{:S(2)}) copy-start(bf16[1,256,1536]{2,1,0:T(8,128)(2,1)} %param.5) | copy-start | bytes 2359300
  2.2 4.0 %collective-permute-start = (bf16[192,1536]{1,0:T(8,128)(2,1)S(1)}, bf16[192,1536]{1,0:T(8,128)(2,1)S(1)}, u32[]{:S(2)}, u32[]{:S(2)}) collective-permute-start(bf16[192,1536]{1,0:T(8,128)(2,1)S(1)} %reshape.16.refs_0_), channel_id=1, source_target_pairs={{0,4},{4,0},{8,12},{12,8},{16,20},{20,16},{24,28},{28,24},{1,5},{5... | collective-permute-start | bytes 1769480 | tf_op jit(solution)/shard_map/ppermute | solution.py:313
  2.3 27.8 %collective-permute-start.2 = (bf16[192,1536]{1,0:T(8,128)(2,1)S(1)}, bf16[192,1536]{1,0:T(8,128)(2,1)S(1)}, u32[]{:S(2)}, u32[]{:S(2)}) collective-permute-start(bf16[192,1536]{1,0:T(8,128)(2,1)S(1)} %reshape.16.refs_0_), channel_id=1, source_target_pairs={{0,16},{4,20},{8,24},{12,28},{16,0},{20,4},{24,8},{28,12},{1,17},{... | collective-permute-start | bytes 1769480 | tf_op jit(solution)/shard_map/ppermute | solution.py:313
  5.0 26.5 %collective-permute-start.1 = (bf16[192,1536]{1,0:T(8,128)(2,1)S(1)}, bf16[192,1536]{1,0:T(8,128)(2,1)S(1)}, u32[]{:S(2)}, u32[]{:S(2)}) collective-permute-start(bf16[192,1536]{1,0:T(8,128)(2,1)S(1)} %reshape.16.refs_0_), channel_id=1, source_target_pairs={{0,8},{4,12},{8,0},{12,4},{16,24},{20,28},{24,16},{28,20},{1,9},{5... | collective-permute-start | bytes 1769480 | tf_op jit(solution)/shard_map/ppermute | solution.py:313
  6.3 26.1 %collective-permute-start.3 = (bf16[192,1536]{1,0:T(8,128)(2,1)S(1)}, bf16[192,1536]{1,0:T(8,128)(2,1)}, u32[]{:S(2)}, u32[]{:S(2)}) collective-permute-start(bf16[192,1536]{1,0:T(8,128)(2,1)S(1)} %collective-permute-done.refs_1_), channel_id=1, source_target_pairs={{0,8},{4,12},{8,0},{12,4},{16,24},{20,28},{24,16},{28,20},{1,9},{5... | collective-permute-start | bytes 1769480 | tf_op jit(solution)/shard_map/ppermute | solution.py:313
  7.8 10.0 %collective-permute-start.7 = (bf16[128,1536]{1,0:T(8,128)(2,1)S(1)}, bf16[128,1536]{1,0:T(8,128)(2,1)S(1)}, u32[]{:S(2)}, u32[]{:S(2)}) collective-permute-start(bf16[128,1536]{1,0:T(8,128)(2,1)S(1)} %get-tuple-element.21), channel_id=1, source_target_pairs={{0,2},{2,3},{3,1},{1,0},{4,6},{6,7},{7,5},{5,4},{8,10},{10,11},{11... | collective-permute-start | bytes 1179656 | tf_op jit(solution)/shard_map/ppermute | solution.py:348
  10.2 16.1 %collective-permute-start.8 = (bf16[128,1536]{1,0:T(8,128)(2,1)S(1)}, bf16[128,1536]{1,0:T(8,128)(2,1)S(1)}, u32[]{:S(2)}, u32[]{:S(2)}) collective-permute-start(bf16[128,1536]{1,0:T(8,128)(2,1)S(1)} %get-tuple-element.20), channel_id=1, source_target_pairs={{0,2},{2,3},{3,1},{1,0},{4,6},{6,7},{7,5},{5,4},{8,10},{10,11},{11... | collective-permute-start | bytes 1179656 | tf_op jit(solution)/shard_map/ppermute | solution.py:348
  17.9 16.9 %collective-permute-start.9 = (bf16[128,1536]{1,0:T(8,128)(2,1)S(1)}, bf16[128,1536]{1,0:T(8,128)(2,1)}, u32[]{:S(2)}, u32[]{:S(2)}) collective-permute-start(bf16[128,1536]{1,0:T(8,128)(2,1)S(1)} %collective-permute-done.7.refs_9_), channel_id=1, source_target_pairs={{0,2},{2,3},{3,1},{1,0},{4,6},{6,7},{7,5},{5,4},{8,10},{10,11},{11... | collective-permute-start | bytes 1179656 | tf_op jit(solution)/shard_map/ppermute | solution.py:348
  26.3 16.9 %collective-permute-start.10 = (bf16[128,1536]{1,0:T(8,128)(2,1)S(1)}, bf16[128,1536]{1,0:T(8,128)(2,1)}, u32[]{:S(2)}, u32[]{:S(2)}) collective-permute-start(bf16[128,1536]{1,0:T(8,128)(2,1)S(1)} %collective-permute-done.8.refs_10_), channel_id=1, source_target_pairs={{0,2},{2,3},{3,1},{1,0},{4,6},{6,7},{7,5},{5,4},{8,10},{10,11},{11... | collective-permute-start | bytes 1179656 | tf_op jit(solution)/shard_map/ppermute | solution.py:348
  30.1 20.8 %collective-permute-start.4 = (bf16[192,1536]{1,0:T(8,128)(2,1)S(1)}, bf16[192,1536]{1,0:T(8,128)(2,1)}, u32[]{:S(2)}, u32[]{:S(2)}) collective-permute-start(bf16[192,1536]{1,0:T(8,128)(2,1)S(1)} %collective-permute-done.refs_1_), channel_id=1, source_target_pairs={{0,16},{4,20},{8,24},{12,28},{16,0},{20,4},{24,8},{28,12},{1,17},{... | collective-permute-start | bytes 1769480 | tf_op jit(solution)/shard_map/ppermute | solution.py:313
  31.5 19.4 %collective-permute-start.5 = (bf16[192,1536]{1,0:T(8,128)(2,1)S(1)}, bf16[192,1536]{1,0:T(8,128)(2,1)}, u32[]{:S(2)}, u32[]{:S(2)}) collective-permute-start(bf16[192,1536]{1,0:T(8,128)(2,1)S(1)} %collective-permute-done.2.refs_3_), channel_id=1, source_target_pairs={{0,8},{4,12},{8,0},{12,4},{16,24},{20,28},{24,16},{28,20},{1,9},{5... | collective-permute-start | bytes 1769480 | tf_op jit(solution)/shard_map/ppermute | solution.py:313
  32.3 22.3 %collective-permute-start.6 = (bf16[192,1536]{1,0:T(8,128)(2,1)}, bf16[192,1536]{1,0:T(8,128)(2,1)}, u32[]{:S(2)}, u32[]{:S(2)}) collective-permute-start(bf16[192,1536]{1,0:T(8,128)(2,1)} %collective-permute-done.3.refs_4_), channel_id=1, source_target_pairs={{0,16},{4,20},{8,24},{12,28},{16,0},{20,4},{24,8},{28,12},{1,17},{... | collective-permute-start | bytes 1769480 | tf_op jit(solution)/shard_map/ppermute | solution.py:313
  34.7 28.1 %collective-permute-start.11 = (bf16[128,1536]{1,0:T(8,128)(2,1)}, bf16[128,1536]{1,0:T(8,128)(2,1)}, u32[]{:S(2)}, u32[]{:S(2)}) collective-permute-start(bf16[128,1536]{1,0:T(8,128)(2,1)} %collective-permute-done.9.refs_11_), channel_id=1, source_target_pairs={{0,2},{2,3},{3,1},{1,0},{4,6},{6,7},{7,5},{5,4},{8,10},{10,11},{11... | collective-permute-start | bytes 1179656 | tf_op jit(solution)/shard_map/ppermute | solution.py:348
  43.1 19.7 %collective-permute-start.12 = (bf16[128,1536]{1,0:T(8,128)(2,1)}, bf16[128,1536]{1,0:T(8,128)(2,1)}, u32[]{:S(2)}, u32[]{:S(2)}) collective-permute-start(bf16[128,1536]{1,0:T(8,128)(2,1)} %collective-permute-done.10.refs_12_), channel_id=1, source_target_pairs={{0,2},{2,3},{3,1},{1,0},{4,6},{6,7},{7,5},{5,4},{8,10},{10,11},{11... | collective-permute-start | bytes 1179656 | tf_op jit(solution)/shard_map/ppermute | solution.py:348
  55.6 7.3 %copy-start.3 = (bf16[128,8,4,128]{3,1,2,0:T(8,128)(2,1)S(1)}, bf16[128,8,4,128]{3,1,2,0:T(8,128)(2,1)}, u32[]{:S(2)}) copy-start(bf16[128,8,4,128]{3,1,2,0:T(8,128)(2,1)} %copy.11) | copy-start | bytes 3145732
  62.8 25.5 %copy-start = (bf16[1536,1536]{1,0:T(8,128)(2,1)}, bf16[1536,1536]{1,0:T(8,128)(2,1)S(1)}, u32[]{:S(2)}) copy-start(bf16[1536,1536]{1,0:T(8,128)(2,1)S(1)} %get-tuple-element.12.w_ref) | copy-start | bytes 14155780
  82.0 1.6 %copy-start.2 = (bf16[1024,512]{1,0:T(8,128)(2,1)}, bf16[1024,512]{1,0:T(8,128)(2,1)S(1)}, u32[]{:S(2)}) copy-start(bf16[1024,512]{1,0:T(8,128)(2,1)S(1)} %get-tuple-element.13) | copy-start | bytes 3145732
  83.7 7.8 %collective-permute-start.16 = (bf16[128,1536]{1,0:T(8,128)(2,1)S(1)}, bf16[128,1536]{1,0:T(8,128)(2,1)S(1)}, u32[]{:S(2)}, u32[]{:S(2)}) collective-permute-start(bf16[128,1536]{1,0:T(8,128)(2,1)S(1)} %products.7), channel_id=1, source_target_pairs={{0,2},{2,3},{3,1},{1,0},{4,6},{6,7},{7,5},{5,4},{8,10},{10,11},{11... | collective-permute-start | bytes 1179656 | tf_op jit(solution)/shard_map/ppermute | solution.py:366
  84.5 14.3 %collective-permute-start.13 = (bf16[128,1536]{1,0:T(8,128)(2,1)S(1)}, bf16[128,1536]{1,0:T(8,128)(2,1)S(1)}, u32[]{:S(2)}, u32[]{:S(2)}) collective-permute-start(bf16[128,1536]{1,0:T(8,128)(2,1)S(1)} %get-tuple-element.17), channel_id=1, source_target_pairs={{0,2},{2,3},{3,1},{1,0},{4,6},{6,7},{7,5},{5,4},{8,10},{10,11},{11... | collective-permute-start | bytes 1179656 | tf_op jit(solution)/shard_map/ppermute | solution.py:363
  91.5 15.7 %collective-permute-start.17 = (bf16[128,1536]{1,0:T(8,128)(2,1)S(1)}, bf16[128,1536]{1,0:T(8,128)(2,1)S(1)}, u32[]{:S(2)}, u32[]{:S(2)}) collective-permute-start(bf16[128,1536]{1,0:T(8,128)(2,1)S(1)} %add_convert_fusion.1), channel_id=1, source_target_pairs={{0,2},{2,3},{3,1},{1,0},{4,6},{6,7},{7,5},{5,4},{8,10},{10,11},{11... | collective-permute-start | bytes 1179656 | tf_op jit(solution)/shard_map/ppermute | solution.py:366
  98.9 16.8 %collective-permute-start.14 = (bf16[128,1536]{1,0:T(8,128)(2,1)S(1)}, bf16[128,1536]{1,0:T(8,128)(2,1)S(1)}, u32[]{:S(2)}, u32[]{:S(2)}) collective-permute-start(bf16[128,1536]{1,0:T(8,128)(2,1)S(1)} %add_convert_fusion.3), channel_id=1, source_target_pairs={{0,2},{2,3},{3,1},{1,0},{4,6},{6,7},{7,5},{5,4},{8,10},{10,11},{11... | collective-permute-start | bytes 1179656 | tf_op jit(solution)/shard_map/ppermute | solution.py:363
  108.0 37.3 %collective-permute-start.18 = (bf16[128,1536]{1,0:T(8,128)(2,1)}, bf16[128,1536]{1,0:T(8,128)(2,1)S(1)}, u32[]{:S(2)}, u32[]{:S(2)}) collective-permute-start(bf16[128,1536]{1,0:T(8,128)(2,1)} %add_convert_fusion), channel_id=1, source_target_pairs={{0,2},{2,3},{3,1},{1,0},{4,6},{6,7},{7,5},{5,4},{8,10},{10,11},{11... | collective-permute-start | bytes 1179656 | tf_op jit(solution)/shard_map/ppermute | solution.py:366
  116.4 28.9 %collective-permute-start.15 = (bf16[128,1536]{1,0:T(8,128)(2,1)}, bf16[128,1536]{1,0:T(8,128)(2,1)}, u32[]{:S(2)}, u32[]{:S(2)}) collective-permute-start(bf16[128,1536]{1,0:T(8,128)(2,1)} %add_convert_fusion.2), channel_id=1, source_target_pairs={{0,2},{2,3},{3,1},{1,0},{4,6},{6,7},{7,5},{5,4},{8,10},{10,11},{11... | collective-permute-start | bytes 1179656 | tf_op jit(solution)/shard_map/ppermute | solution.py:363
  141.6 2.3 %copy-start.1 = (bf16[1536,1536]{1,0:T(8,128)(2,1)S(1)}, bf16[1536,1536]{1,0:T(8,128)(2,1)}, u32[]{:S(2)}) copy-start(bf16[1536,1536]{1,0:T(8,128)(2,1)} %copy-done) | copy-start | bytes 14155780
  (2 other events, 1.7 us)
